TPU v7x, 512 devices: a whole 4x8x8 slice. The times are simulated.
512 devices in a mesh: pb: 16 (over y, core), ka: 32 (over x, z).
Axes of the slice: x: 4, y: 8, z: 8, core: 2. Of those that a mesh axis runs over, the one named last changes fastest.
Arguments:
- coupling: bfloat16 [16, 1728, 2, 1600], P('pb', 'ka'), may hold values from -6 to 6
- rot_k: bfloat16 [1728, 2, 1600], P('ka'), may hold values from -0.625 to 0.625
- rot_kq: bfloat16 [16, 1728, 2, 1600], P('pb', 'ka'), may hold values from -0.625 to 0.625
- r_elec: int32 [2048, 3], replicated, may hold values from -6 to 6
- degen: int32 [2048], replicated, may hold values from 1 to 8
- reader: int32 [2048, 1], replicated, may hold values from 0 to 31; in each aligned block of 2048 rows (0 to 2047, 2048 to 4095, ...) at most 128 rows name the same one
- r_phon: int32 [32, 3], replicated, may hold values from -3 to 3
Outputs:
- wannier: float32 [32, 2, 1600, 4096], P(None, None, 'pb', 'ka')
Inputs may be any that keep to these rules, and one draw needn't show every extreme that they name: Each reader is named by at most 128 lattice vectors, and one reader by exactly 128.
All inputs are finite; a program needn't handle non-finite values.
Results may differ from a plain program's by a relative error of at most 0.0056.
Values may be sent and summed in bfloat16 or wider, within the bound.
A program may use at most 128 MiB of HBM per device.

v0:
```python
import math
import jax
import jax.numpy as jnp
from jax import lax
from jax.sharding import PartitionSpec as P

W = 40
KGRID = 12
QGRID = 6


def angle_tables(vectors, count, grid):
    index = jnp.arange(count, dtype=jnp.int32)
    first = index // (grid * grid)
    second = index // grid % grid
    third = index % grid
    inner = (
        vectors[:, 0:1] * first[None, :]
        + vectors[:, 1:2] * second[None, :]
        + vectors[:, 2:3] * third[None, :]
    )
    angle = jnp.mod(inner, grid).astype(jnp.float32) * (2.0 * math.pi / grid)
    return (jnp.cos(angle).astype(jnp.bfloat16), jnp.sin(angle).astype(jnp.bfloat16))


def slot_tables(reader, degen, readers, most):
    reader_row = reader[:, 0]
    member = (reader_row[:, None] == jnp.arange(readers, dtype=jnp.int32)[None, :]).astype(
        jnp.int32
    )
    ranking = jnp.sum((jnp.cumsum(member, axis=0) - 1) * member, axis=1)
    position = reader_row * most + ranking
    source_row = (
        jnp.full((readers * most,), -1, jnp.int32)
        .at[position]
        .set(jnp.arange(reader_row.shape[0], dtype=jnp.int32))
    )
    usable = source_row >= 0
    source_row = jnp.maximum(source_row, 0)
    inverse_deg = jnp.where(usable, 1.0 / degen[source_row].astype(jnp.float32), jnp.float32(0.0))
    return (position, source_row, usable, inverse_deg)


def product(spec, left, right):
    return jnp.einsum(spec, left, right, preferred_element_type=jnp.float32)


def rotate(coupling, rot_k, rot_kq):
    q_local, k_local = (coupling.shape[0], coupling.shape[1])
    g_mat = coupling.reshape(q_local, k_local, 2, W, W)
    u_mat = rot_k.reshape(k_local, 2, W, W)
    v_mat = rot_kq.reshape(q_local, k_local, 2, W, W)
    spec = "qkab,kbn->qkan"
    x_real = product(spec, g_mat[:, :, 0], u_mat[:, 0]) - product(spec, g_mat[:, :, 1], u_mat[:, 1])
    x_imag = product(spec, g_mat[:, :, 0], u_mat[:, 1]) + product(spec, g_mat[:, :, 1], u_mat[:, 0])
    x_real = x_real.astype(jnp.bfloat16)
    x_imag = x_imag.astype(jnp.bfloat16)
    spec_two = "qkam,qkan->qkmn"
    y_real = product(spec_two, v_mat[:, :, 0], x_real) + product(spec_two, v_mat[:, :, 1], x_imag)
    y_imag = product(spec_two, v_mat[:, :, 0], x_imag) - product(spec_two, v_mat[:, :, 1], x_real)
    return jnp.stack([y_real, y_imag], 2).reshape(q_local, k_local, 2, W * W).astype(jnp.bfloat16)


def per_device(coupling, rot_k, rot_kq, r_elec, degen, reader, r_phon):
    ka_count = lax.axis_size("ka")
    pb_count = lax.axis_size("pb")
    q_local, k_local, width_sq = (coupling.shape[0], coupling.shape[1], coupling.shape[3])
    total_k = k_local * ka_count
    total_r = r_elec.shape[0]
    most = 2 * total_r // ka_count
    scale = total_k ** (-0.5)
    rotated = rotate(coupling, rot_k, rot_kq)
    position, source_row, usable, inverse_deg = slot_tables(reader, degen, ka_count, most)
    offset = lax.axis_index("ka") * most
    my_rows = lax.dynamic_slice_in_dim(source_row, offset, most)
    my_usable = lax.dynamic_slice_in_dim(usable, offset, most)
    my_vectors = r_elec[my_rows]
    keep = my_usable.astype(jnp.bfloat16)[:, None]
    span = q_local * width_sq
    piece = lax.all_gather(rotated, "ka", axis=1, tiled=True)
    count = piece.shape[1]
    cosine, sine = angle_tables(my_vectors, count, KGRID)
    left = jnp.concatenate([cosine * keep, sine * keep], axis=1)
    z_real = piece[:, :, 0].transpose(1, 0, 2).reshape(count, span)
    z_imag = piece[:, :, 1].transpose(1, 0, 2).reshape(count, span)
    upper = jnp.concatenate([z_real, z_imag], axis=1)
    lower = jnp.concatenate([z_imag, -z_real], axis=1)
    right = jnp.concatenate([upper, lower], axis=0)
    summed = jnp.dot(left, right, preferred_element_type=jnp.float32)
    real_sum = summed[:, :span]
    imag_sum = summed[:, span:]
    stacked = jnp.stack(
        [real_sum.reshape(most, q_local, width_sq), imag_sum.reshape(most, q_local, width_sq)], 2
    )
    mine = (stacked * scale).astype(jnp.bfloat16)
    gathered_q = lax.all_to_all(mine, "pb", split_axis=3, concat_axis=1, tiled=True)
    total_q = q_local * pb_count
    slim = gathered_q.shape[3]
    phonon_count = r_phon.shape[0]
    q_cos, q_sin = angle_tables(r_phon, total_q, QGRID)
    flat = gathered_q.transpose(1, 0, 2, 3).reshape(total_q, most * 2 * slim)
    c_part = jnp.dot(q_cos, flat, preferred_element_type=jnp.float32).reshape(
        phonon_count, most, 2, slim
    )
    s_part = jnp.dot(q_sin, flat, preferred_element_type=jnp.float32).reshape(
        phonon_count, most, 2, slim
    )
    real_out = c_part[:, :, 0] + s_part[:, :, 1]
    imag_out = c_part[:, :, 1] - s_part[:, :, 0]
    result = jnp.stack([real_out, imag_out], 1).transpose(0, 1, 3, 2)
    my_inverse = lax.dynamic_slice_in_dim(inverse_deg, offset, most)
    return result * (my_inverse * total_q ** (-0.5))[None, None, None, :]


def solution(mesh):
    in_specs = (
        P("pb", "ka", None, None),
        P("ka", None, None),
        P("pb", "ka", None, None),
        P(),
        P(),
        P(),
        P(),
    )
    out_specs = P(None, None, "pb", "ka")
    return jax.shard_map(
        per_device, mesh=mesh, in_specs=in_specs, out_specs=out_specs, check_vma=False
    )
```

profile of v0, /device:TPU:1, one launch (start us, length us, event | category | flops | bytes accessed | tf_op | source)
XLA Modules:
  0.0 320.0 jit_solution(17944751337558424967)
XLA Ops:
  6.5 1.1 copy.55
  7.6 1.0 reshape.274
  8.7 1.7 reshape.311
  10.3 0.5 fusion.28
  10.8 1.5 fusion.29
  12.3 1.3 fusion.19
  13.6 0.8 copy.57
  14.4 2.0 reshape.278
  16.4 1.8 fusion.18
  18.3 0.4 fusion.31
  18.7 0.4 fusion.30
  19.2 0.5 fusion.17
  19.6 1.0 copy.58
  20.7 1.5 stack.21
  22.2 0.5 fusion.16
  22.7 0.3 copy.59
  23.0 0.5 stack.22
  23.5 1.0 copy.60
  24.6 9.1 %reduce-window.6 = s32[32,16,128]{2,1,0:T(8,128)S(1)} reduce-window(s32[32,16,128]{2,1,0:T(8,128)S(1)} %fusion.36, s32[]{:T(128)} %constant.88.clone.1), window={size=1x1x128 pad=0_0x0_0x127_0}, to_apply=%region_0.0 | reduce-window | flops 8323072 | bytes 524292 | tf_op jit(solution)/shard_map/reduce-window
  33.7 0.1 slice.98
  33.8 0.2 copy.74
  34.1 0.2 reduce-window.9
  34.3 0.4 copy.52
  34.6 0.1 add_add_fusion
  34.9 8.2 %scatter_custom_fusion = s32[4096]{0:T(1024)S(1)} fusion(s32[2048]{0:T(1024)S(1)} %bitcast.125, s32[2048]{0:T(1024)S(1)} %iota.45, s32[]{:T(128)} %constant.90.clone.1), kind=kCustom, calls=%fused_computation.94 | custom fusion | bytes 16388 | tf_op jit(solution)/shard_map/scatter | solution.py:36
  43.3 0.6 gather_fusion
  44.0 0.2 slice_reduce_fusion.2
  44.2 4.3 %fusion.32 = (bf16[128,1728]{1,0:T(8,128)(2,1)S(1)}, bf16[128,1728]{1,0:T(8,128)(2,1)S(1)}) fusion(s32[1728]{0:T(1024)S(1)} %get-tuple-element.21, s32[128]{0:T(128)S(1)} %get-tuple-element.7, s32[1728]{0:T(1024)S(1)} %get-tuple-element.22, s32[128]{0:T(128)S(1)} %get-tuple-element.6, s32[1728]{0:T(1024)S(1)} %add_select_fusion.4, ...), kind=kLoop, calls=%fused_computation.56 | loop fusion | flops 4866048 | bytes 907264 | tf_op jit(solution)/shard_map/mul | solution.py:83
  48.5 100.7 %all-gather.2.cloned.1.call-done = bf16[1,1728,2,1600]{3,2,0,1:T(2,128)(2,1)} async-done(((bf16[1,54,2,1600]{3,2,0,1:T(2,128)(2,1)}), bf16[1,1728,2,1600]{3,2,0,1:T(2,128)(2,1)}) %all-gather.2.cloned.1.call-update) | async-done | bytes 11059216 | tf_op jit(solution)/shard_map/all_gather | solution.py:80
  149.2 23.0 %fusion.69 = (bf16[1,1728,1,1600]{3,2,0,1:T(2,128)(2,1)}, bf16[1,1728,1,1600]{3,2,0,1:T(2,128)(2,1)}) fusion(bf16[1,1728,2,1600]{3,2,0,1:T(2,128)(2,1)} %all-gather.2.cloned.1.call-done), kind=kLoop, calls=%fused_computation.131 | loop fusion | bytes 22118400 | tf_op jit(solution)/shard_map/slice | solution.py:85
  172.2 25.3 %copy.80 = bf16[1,1728,1,1600]{1,3,2,0:T(8,128)(2,1)} copy(bf16[1,1728,1,1600]{3,2,0,1:T(2,128)(2,1)} %get-tuple-element.9) | data formatting | bytes 11059200
  197.5 5.4 %bitcast_negate_fusion = bf16[1728,1600]{0,1:T(8,128)(2,1)} fusion(bf16[1,1728,1,1600]{1,3,2,0:T(8,128)(2,1)} %copy.80), kind=kLoop, calls=%fused_computation.124 | loop fusion | flops 2764800 | bytes 11059200 | tf_op jit(solution)/shard_map/neg | solution.py:87
  202.9 25.2 %copy.81 = bf16[1,1728,1,1600]{1,3,2,0:T(8,128)(2,1)} copy(bf16[1,1728,1,1600]{3,2,0,1:T(2,128)(2,1)} %get-tuple-element.8) | data formatting | bytes 11059200
  228.1 30.9 %fusion = f32[128,3200]{0,1:T(8,128)S(1)} fusion(bf16[1728,1600]{0,1:T(8,128)(2,1)} %bitcast_negate_fusion, bf16[1728,1600]{0,1:T(8,128)(2,1)} %bitcast.115, bf16[1728,1600]{0,1:T(8,128)(2,1)} %bitcast.114, bf16[128,1728]{1,0:T(8,128)(2,1)S(1)} %get-tuple-element.15, bf16[128,1728]{1,0:T(8,128)(2,1)S(1)} %get-tuple-element.14), kind=kOutput, calls=%fused_computation.3 | convolution fusion | flops 2921398272 | bytes 19111936 | tf_op jit(solution)/shard_map/dot_general | solution.py:89
  259.1 0.2 fusion.11
  259.3 7.8 %copy.65 = bf16[128,1,2,1600]{0,2,1,3:T(2,128)(2,1)} copy(bf16[128,1,2,1600]{0,3,2,1:T(8,128)(2,1)S(1)} %fusion.11) | data formatting | bytes 1638400 | tf_op jit(solution)/shard_map/convert_element_type | solution.py:95
  267.0 8.0 %all-to-all-start = ((bf16[128,1,2,1600]{0,2,1,3:T(2,128)(2,1)}), bf16[128,1,2,1600]{0,2,1,3:T(2,128)(2,1)S(1)}, u32[]{:S(2)}, u32[]{:S(2)}) async-start(bf16[128,1,2,1600]{0,2,1,3:T(2,128)(2,1)} %copy.65), calls=%async_computation | async-start | bytes 1638400 | tf_op jit(solution)/shard_map/all_to_all | solution.py:96
  275.0 23.0 %gather_fusion.1 = s32[4096]{0:T(1024)S(1)} fusion(s32[2048]{0:T(1024)S(1)} %copy-done, s32[4096]{0:T(1024)S(1)} %get-tuple-element.16), kind=kCustom, calls=%fused_computation.1 | custom fusion | bytes 49152 | tf_op jit(solution)/shard_map/gather | solution.py:40
  298.2 0.2 all-to-all-done
  298.5 0.8 copy.67
  299.4 2.0 reshape.282
  301.4 4.0 %dot_general.47 = bf16[128,2,100,16]{2,1,0,3:T(2,128)(2,1)S(1)} reshape(bf16[25600,16]{0,1:T(8,128)(2,1)S(1)} %bitcast.117) | data formatting | bytes 1638400 | tf_op jit(solution)/shard_map/dot_general | solution.py:102
  305.4 0.9 copy.68
  306.2 0.7 fusion.53
  307.0 0.7 fusion.56
  307.7 0.8 fusion.10
  308.5 0.4 fusion.8
  308.9 4.2 %copy.70 = f32[32,2,100,128]{3,1,2,0:T(2,128)} copy(f32[32,2,100,128]{3,0,2,1:T(8,128)S(1)} %fusion.8) | data formatting | bytes 6553600 | tf_op jit(solution)/shard_map/mul | solution.py:112
  (36 shorter events, 0.8 us)
Async XLA Ops:
  6.5 268.5 %copy-start = (s32[2048]{0:T(1024)S(1)}, s32[2048]{0:T(1024)}, u32[]{:S(2)}) copy-start(s32[2048]{0:T(1024)} %param.11) | copy-start | bytes 24580
  6.5 2.1 copy-start.3
  6.5 142.7 %all-gather.2.cloned.1.call-start = ((), (), s32[]{:S(2)}) async-start(), calls=%async_computation.1 | async-start | bytes 11860992 | tf_op jit(solution)/shard_map/all_gather | solution.py:80
  12.3 1.3 copy-start.4
  16.4 1.8 copy-start.1
  19.2 3.1 copy-start.2
  22.7 1.9 copy-start.5
  23.4 10.8 %copy-start.6 = (s32[2048,3]{0,1:T(4,128)S(1)}, s32[2048,3]{0,1:T(4,128)}, u32[]{:S(2)}) copy-start(s32[2048,3]{0,1:T(4,128)} %param.10) | copy-start | bytes 73732
  267.0 31.4 %all-to-all-start = ((bf16[128,1,2,1600]{0,2,1,3:T(2,128)(2,1)}), bf16[128,1,2,1600]{0,2,1,3:T(2,128)(2,1)S(1)}, u32[]{:S(2)}, u32[]{:S(2)}) async-start(bf16[128,1,2,1600]{0,2,1,3:T(2,128)(2,1)} %copy.65), calls=%async_computation | async-start | bytes 1638400 | tf_op jit(solution)/shard_map/all_to_all | solution.py:96
  275.0 23.2 %copy-start.7 = (s32[32,3]{0,1:T(4,128)S(1)}, s32[32,3]{0,1:T(4,128)}, u32[]{:S(2)}) copy-start(s32[32,3]{0,1:T(4,128)} %param.13) | copy-start | bytes 1156
Sparse Core Ops, SparseCore 0:
  24.7 124.4 all-gather.1
where the time goes:
time: 322 us; the launch traced here: 320 us
  local copies, waits for them, and re-layouts  137 us (43%)
  waiting for transfers between devices  101 us (31%)
  matrix products  39.3 us (12%)
  other arithmetic  21 us (7%)
  between operations  13.8 us (4%)
  starting transfers between devices  7.98 us (2%)
    all_gather x1, waiting for transfers between devices, per_device(): piece = lax.all_gather(rotated, 'ka', axis=1, tiled=True)  101 us
    unnamed x21, local copies, waits for them, and re-layouts  52.7 us
    dot_general x1, matrix products, per_device(): summed = jnp.dot(left, right, preferred_element_type=jnp.float32)  30.9 us
    gather x1, local copies, waits for them, and re-layouts, slot_tables(): degen[source_row].astype(jnp.float32)  23 us
    slice x1, local copies, waits for them, and re-layouts, per_device(): z_imag = piece[:, :, 1].transpose(1, 0, 2).reshape(count, span)  23 us
    another operation x2, other arithmetic  9.27 us
    scatter x1, local copies, waits for them, and re-layouts, slot_tables(): source_row = jnp.full((readers * most,), -1, jnp.int32).at[position].set(...  8.24 us
    all_to_all x1, starting transfers between devices, per_device(): lax.all_to_all(mine, 'pb', split_axis=3, concat_axis=1, tiled=True)  7.97 us
  transfers between devices with their start and end apart: 2, of which 2 were waited for; matrix products, arithmetic and copies ran while one was open for 15% of the time, Pallas kernels for 0%

commit v1 on v0

--- a/solution.py
+++ b/solution.py
@@ -77,7 +77,8 @@
     my_vectors = r_elec[my_rows]
     keep = my_usable.astype(jnp.bfloat16)[:, None]
     span = q_local * width_sq
-    piece = lax.all_gather(rotated, "ka", axis=1, tiled=True)
+    repeated = jnp.stack([rotated] * lax.axis_size("ka"))
+    piece = jnp.concatenate(lax.all_to_all(repeated, "ka", 0, 0), axis=1)
     count = piece.shape[1]
     cosine, sine = angle_tables(my_vectors, count, KGRID)
     left = jnp.concatenate([cosine * keep, sine * keep], axis=1)

time: 322 us -> 479 us (1.49)
  the two profiles are of different devices: /device:TPU:1 before, /device:TPU:135 now
where the time goes in v1:
time: 479 us; the launch traced here: 470 us
  waiting for transfers between devices  238 us (50%)
  local copies, waits for them, and re-layouts  112 us (23%)
  matrix products  72.7 us (15%)
  other arithmetic  25.2 us (5%)
  starting transfers between devices  21.5 us (4%)
    all_to_all x1, waiting for transfers between devices, per_device(): piece = jnp.concatenate(lax.all_to_all(repeated, 'ka', 0, 0), axis=1)  238 us
    dot_general x1, matrix products, per_device(): summed = jnp.dot(left, right, preferred_element_type=jnp.float32)  64.3 us
    gather x1, local copies, waits for them, and re-layouts, slot_tables(): degen[source_row].astype(jnp.float32)  23 us
    slice x1, local copies, waits for them, and re-layouts, per_device(): z_imag = piece[:, :, 1].transpose(1, 0, 2).reshape(count, span)  23 us
    scatter x1, local copies, waits for them, and re-layouts, slot_tables(): source_row = jnp.full((readers * most,), -1, jnp.int32).at[position].set(...  20.2 us
    all_to_all x1, starting transfers between devices, per_device(): piece = jnp.concatenate(lax.all_to_all(repeated, 'ka', 0, 0), axis=1)  11.3 us
    all_to_all x1, starting transfers between devices, per_device(): lax.all_to_all(mine, 'pb', split_axis=3, concat_axis=1, tiled=True)  10.2 us
    neg x1, other arithmetic, per_device(): lower = jnp.concatenate([z_imag, -z_real], axis=1)  9.64 us
  transfers between devices with their start and end apart: 2, of which 2 were waited for; matrix products, arithmetic and copies ran while one was open for 13% of the time, Pallas kernels for 0%

profile of v1, /device:TPU:135, one launch (start us, length us, event | category | flops | bytes accessed | tf_op | source)
XLA Modules:
  0.0 470.0 jit_solution(4981670677058924108)
XLA Ops:
  0.0 1.1 copy.73
  1.1 1.0 reshape.273
  2.1 1.7 reshape.311
  3.8 0.5 fusion.23
  4.3 1.5 fusion.24
  5.8 1.3 fusion.14
  7.1 0.8 copy.75
  7.9 2.0 reshape.277
  9.9 1.8 fusion.13
  11.7 0.5 fusion.26
  12.2 0.4 fusion.25
  12.7 0.5 fusion.12
  13.1 1.0 copy.76
  14.2 1.5 stack.16
  15.7 0.5 fusion.11
  16.2 0.3 copy.77
  16.5 0.5 stack.17
  17.0 0.3 copy.78
  17.3 7.6 %stack.19 = bf16[32,1,54,2,1600]{4,3,2,1,0:T(2,128)(2,1)} broadcast(bf16[54,2,1600]{2,1,0:T(2,128)(2,1)S(1)} %copy.78), dimensions={2,3,4} | broadcast | bytes 11404800 | tf_op jit(solution)/shard_map/stack | solution.py:80
  24.9 11.3 %all-to-all-start = ((bf16[32,1,54,2,1600]{4,3,2,1,0:T(2,128)(2,1)}), bf16[32,1,54,2,1600]{4,3,2,1,0:T(2,128)(2,1)}, u32[]{:S(2)}, u32[]{:S(2)}) async-start(bf16[32,1,54,2,1600]{4,3,2,1,0:T(2,128)(2,1)} %stack.19), calls=%async_computation | async-start | bytes 23003136 | tf_op jit(solution)/shard_map/all_to_all | solution.py:81
  36.2 9.1 %reduce-window.6 = s32[32,16,128]{2,1,0:T(8,128)S(1)} reduce-window(s32[32,16,128]{2,1,0:T(8,128)S(1)} %fusion.31, s32[]{:T(128)} %constant.88.clone.1), window={size=1x1x128 pad=0_0x0_0x127_0}, to_apply=%region_0.0 | reduce-window | flops 8323072 | bytes 524292 | tf_op jit(solution)/shard_map/reduce-window
  45.4 0.2 copy.94
  45.7 0.2 reduce-window.9
  45.9 0.4 copy.70
  46.5 20.2 %scatter_custom_fusion = s32[4096]{0:T(1024)S(1)} fusion(s32[2048]{0:T(1024)S(1)} %bitcast.130, s32[2048]{0:T(1024)S(1)} %iota.45, s32[]{:T(128)} %constant.90.clone.1), kind=kCustom, calls=%fused_computation.92 | custom fusion | bytes 16388 | tf_op jit(solution)/shard_map/scatter | solution.py:36
  66.9 0.6 gather_fusion
  67.7 0.2 slice_reduce_fusion.2
  67.9 4.3 fusion.27
  72.2 237.8 %all-to-all-done = bf16[32,1,54,2,1600]{4,3,2,1,0:T(2,128)(2,1)} async-done(((bf16[32,1,54,2,1600]{4,3,2,1,0:T(2,128)(2,1)}), bf16[32,1,54,2,1600]{4,3,2,1,0:T(2,128)(2,1)}, u32[]{:S(2)}, u32[]{:S(2)}) %all-to-all-start) | async-done | bytes 11059232 | tf_op jit(solution)/shard_map/all_to_all | solution.py:81
  309.9 23.0 %fusion.65 = (bf16[1,1728,1,1600]{3,2,1,0:T(2,128)(2,1)}, bf16[1,1728,1,1600]{3,2,1,0:T(2,128)(2,1)}) fusion(bf16[1,1728,2,1600]{3,2,1,0:T(2,128)(2,1)} %bitcast.30), kind=kLoop, calls=%fused_computation.129 | loop fusion | bytes 22118400 | tf_op jit(solution)/shard_map/slice | solution.py:86
  332.9 9.6 %fusion.64 = (bf16[1728,1600]{1,0:T(8,128)(2,1)}, bf16[1728,1600]{1,0:T(8,128)(2,1)}) fusion(bf16[1,1728,1,1600]{3,2,1,0:T(2,128)(2,1)} %get-tuple-element.11), kind=kLoop, calls=%fused_computation.128 | loop fusion | flops 2764800 | bytes 16588800 | tf_op jit(solution)/shard_map/neg | solution.py:88
  342.6 5.2 %copy.111 = bf16[1,1728,1,1600]{3,1,2,0:T(8,128)(2,1)S(1)} copy(bf16[1,1728,1,1600]{3,2,1,0:T(2,128)(2,1)} %get-tuple-element.10) | data formatting | bytes 11059200
  347.7 64.3 %fusion.1 = f32[128,3200]{0,1:T(8,128)} fusion(bf16[1728,1600]{1,0:T(8,128)(2,1)} %get-tuple-element.8, bf16[1728,1600]{1,0:T(8,128)(2,1)S(1)} %bitcast.120, bf16[1728,1600]{1,0:T(8,128)(2,1)} %get-tuple-element.9, bf16[128,1728]{1,0:T(8,128)(2,1)S(1)} %get-tuple-element.17, bf16[128,1728]{1,0:T(8,128)(2,1)S(1)} %get-tuple-element.16), kind=kOutput, calls=%fused_computation.6 | convolution fusion | flops 2921398272 | bytes 19111936 | tf_op jit(solution)/shard_map/dot_general | solution.py:90
  412.1 1.5 slice_bitcast_fusion.1
  413.6 0.2 fusion.6
  413.8 7.5 %copy.85 = bf16[128,1,2,1600]{0,2,1,3:T(2,128)(2,1)} copy(bf16[128,1,2,1600]{0,3,2,1:T(8,128)(2,1)S(1)} %fusion.6) | data formatting | bytes 1638400 | tf_op jit(solution)/shard_map/convert_element_type | solution.py:96
  421.3 10.2 %all-to-all-start.1 = ((bf16[128,1,2,1600]{0,2,1,3:T(2,128)(2,1)}), bf16[128,1,2,1600]{0,2,1,3:T(2,128)(2,1)S(1)}, u32[]{:S(2)}, u32[]{:S(2)}) async-start(bf16[128,1,2,1600]{0,2,1,3:T(2,128)(2,1)} %copy.85), calls=%async_computation.1 | async-start | bytes 1638400 | tf_op jit(solution)/shard_map/all_to_all | solution.py:97
  431.5 23.0 %gather_fusion.1 = s32[4096]{0:T(1024)S(1)} fusion(s32[2048]{0:T(1024)S(1)} %copy-done, s32[4096]{0:T(1024)S(1)} %get-tuple-element.18), kind=kCustom, calls=%fused_computation.1 | custom fusion | bytes 49152 | tf_op jit(solution)/shard_map/gather | solution.py:40
  454.7 0.2 all-to-all-done.1
  455.0 0.8 copy.87
  455.8 2.0 reshape.282
  457.9 4.0 dot_general.47
  461.8 0.9 copy.88
  462.7 0.7 fusion.48
  463.4 0.7 fusion.51
  464.2 0.8 fusion.5
  465.0 0.4 fusion.3
  465.4 4.2 copy.90
  (35 shorter events, 0.9 us)
Async XLA Ops:
  0.0 431.5 %copy-start = (s32[2048]{0:T(1024)S(1)}, s32[2048]{0:T(1024)}, u32[]{:S(2)}) copy-start(s32[2048]{0:T(1024)} %param.11) | copy-start | bytes 24580
  0.0 2.1 copy-start.3
  5.8 1.3 copy-start.4
  9.9 1.8 copy-start.1
  12.7 3.1 copy-start.2
  24.9 11.3 %copy-start.5 = (s32[2048,1]{0,1:T(1,128)S(1)}, s32[2048,1]{0,1:T(1,128)}, u32[]{:S(2)}) copy-start(s32[2048,1]{0,1:T(1,128)} %param.12) | copy-start | bytes 24580
  24.9 285.0 %all-to-all-start = ((bf16[32,1,54,2,1600]{4,3,2,1,0:T(2,128)(2,1)}), bf16[32,1,54,2,1600]{4,3,2,1,0:T(2,128)(2,1)}, u32[]{:S(2)}, u32[]{:S(2)}) async-start(bf16[32,1,54,2,1600]{4,3,2,1,0:T(2,128)(2,1)} %stack.19), calls=%async_computation | async-start | bytes 23003136 | tf_op jit(solution)/shard_map/all_to_all | solution.py:81
  36.2 9.7 %copy-start.6 = (s32[2048,3]{0,1:T(4,128)S(1)}, s32[2048,3]{0,1:T(4,128)}, u32[]{:S(2)}) copy-start(s32[2048,3]{0,1:T(4,128)} %param.10) | copy-start | bytes 73732
  421.3 33.6 %all-to-all-start.1 = ((bf16[128,1,2,1600]{0,2,1,3:T(2,128)(2,1)}), bf16[128,1,2,1600]{0,2,1,3:T(2,128)(2,1)S(1)}, u32[]{:S(2)}, u32[]{:S(2)}) async-start(bf16[128,1,2,1600]{0,2,1,3:T(2,128)(2,1)} %copy.85), calls=%async_computation.1 | async-start | bytes 1638400 | tf_op jit(solution)/shard_map/all_to_all | solution.py:97
  431.5 23.2 %copy-start.7 = (s32[32,3]{0,1:T(4,128)S(1)}, s32[32,3]{0,1:T(4,128)}, u32[]{:S(2)}) copy-start(s32[32,3]{0,1:T(4,128)} %param.13) | copy-start | bytes 1156
